TPU v7x, 256 devices: a whole 4x4x8 slice. The times are simulated.
256 devices in a mesh: dp: 8 (over z_lo, core), expert: 32 (over x, z_hi, y).
Axes of the slice: x: 4, y: 4, z: 8 (z_hi: 2, z_lo: 4; z = z_hi * 4 + z_lo), core: 2. Of those that a mesh axis runs over, the one named last changes fastest.
Arguments:
- tokens: bfloat16 [16384, 2048], P(('dp', 'expert')), may hold values from -6 to 6
- routes: int32 [16384, 8], P(('dp', 'expert')), may hold values from 0 to 63, all different within a row; in each aligned block of 64 rows (0 to 63, 64 to 127, ...) at most 12 rows name the same one
- route_weight: int32 [16384, 8], P(('dp', 'expert')), may hold values from 1 to 65535
- capacity: int32 [64], replicated, may hold values from 8 to 10
- hot_expert: int32 [1], replicated, may hold values from 0 to 63
- w_gate: bfloat16 [64, 2048, 768], P('expert', 'dp'), may hold values from -0.125 to 0.125
- w_up: bfloat16 [64, 2048, 768], P('expert', 'dp'), may hold values from -0.125 to 0.125
- w_down: bfloat16 [64, 768, 2048], P('expert', None, 'dp'), may hold values from -0.21875 to 0.21875
Outputs:
- mixed: bfloat16 [16384, 2048], P(('dp', 'expert'))
All inputs are finite; a program needn't handle non-finite values.
Results may differ from a plain program's by a relative error of at most 0.0057.
Values may be sent and summed in bfloat16 or wider, within the bound.
No kernel may reach another device: no remote copies, remote signals or barrier semaphores. Data moves between devices by JAX's collectives and lax.ppermute only.
A program may use at most 128 MiB of HBM per device.

v0:
```python
import jax
import jax.numpy as jnp
from jax import lax
from jax.sharding import PartitionSpec as P

CAP = 10
MOST = 12


def per_device(tokens, routes, route_weight, capacity, hot_expert, w_gate, w_up, w_down):
    tok_rows = tokens.shape[0]
    width = tokens.shape[1]
    n_peer = lax.axis_size("expert")
    my_index = lax.axis_index("expert")
    exp_dev = w_gate.shape[0]
    experts = exp_dev * n_peer
    flat_e = routes.reshape(-1)
    weights = route_weight.astype(jnp.float32)
    share = (weights / jnp.sum(weights, axis=1, keepdims=True)).reshape(-1)
    onehot = (flat_e[:, None] == jnp.arange(experts, dtype=jnp.int32)[None, :]).astype(jnp.int32)
    before = jnp.cumsum(onehot, axis=0) - onehot
    rank = jnp.sum(onehot * before, axis=1)
    cap_of = jnp.sum(onehot * capacity[None, :], axis=1)
    hot = hot_expert[0]
    owner = hot // exp_dev
    hot_local = jnp.clip(hot - my_index * exp_dev, 0, exp_dev - 1)
    is_hot = flat_e == hot
    kept_cap = jnp.logical_and(jnp.logical_not(is_hot), rank < cap_of)
    target_cap = jnp.where(kept_cap, flat_e * CAP + rank, -1).reshape(tok_rows, -1)
    target_hot = jnp.where(is_hot, rank, -1).reshape(tok_rows, -1)
    select_cap = jnp.any(
        target_cap[None, :, :] == jnp.arange(experts * CAP, dtype=jnp.int32)[:, None, None], axis=2
    ).astype(jnp.bfloat16)
    select_hot = jnp.any(
        target_hot[None, :, :] == jnp.arange(MOST, dtype=jnp.int32)[:, None, None], axis=2
    ).astype(jnp.bfloat16)
    send_cap = jnp.dot(select_cap, tokens, preferred_element_type=jnp.float32).astype(jnp.bfloat16)
    send_cap = send_cap.reshape(n_peer, exp_dev * CAP, width)
    hot_rows = jnp.dot(select_hot, tokens, preferred_element_type=jnp.float32).astype(jnp.bfloat16)
    cap_slots = exp_dev * CAP
    owner_mask = (jnp.arange(n_peer, dtype=jnp.int32) == owner)[:, None, None]
    send_hot = jnp.where(owner_mask, hot_rows[None, :, :], jnp.zeros((), jnp.bfloat16))
    received = lax.all_to_all(
        jnp.concatenate([send_cap, send_hot], axis=1),
        "expert",
        split_axis=0,
        concat_axis=0,
        tiled=True,
    )
    recv_cap = received[:, :cap_slots].reshape(n_peer, exp_dev, CAP, width)
    recv_hot = received[:, cap_slots:]
    piece_gate = lax.all_gather(w_gate, "dp", axis=1, tiled=True)
    piece_up = lax.all_gather(w_up, "dp", axis=1, tiled=True)
    hot_gate = lax.dynamic_index_in_dim(piece_gate, hot_local, 0, keepdims=False)
    hot_up = lax.dynamic_index_in_dim(piece_up, hot_local, 0, keepdims=False)
    gate_cap = jnp.einsum(
        "pcrd,cdf->pcrf", recv_cap, piece_gate, preferred_element_type=jnp.float32
    )
    up_cap = jnp.einsum("pcrd,cdf->pcrf", recv_cap, piece_up, preferred_element_type=jnp.float32)
    gate_hot = jnp.einsum("prd,df->prf", recv_hot, hot_gate, preferred_element_type=jnp.float32)
    up_hot = jnp.einsum("prd,df->prf", recv_hot, hot_up, preferred_element_type=jnp.float32)
    gate_cap, up_cap, gate_hot, up_hot = (gate_cap, up_cap, gate_hot, up_hot)
    hidden_cap = (jax.nn.silu(gate_cap) * up_cap).astype(jnp.bfloat16)
    hidden_hot = (jax.nn.silu(gate_hot) * up_hot).astype(jnp.bfloat16)
    piece = lax.all_gather(w_down, "dp", axis=2, tiled=True)
    count = piece.shape[2]
    hot_down = lax.dynamic_index_in_dim(piece, hot_local, 0, keepdims=False)
    out_cap = jnp.einsum("pcrf,cfd->pcrd", hidden_cap, piece, preferred_element_type=jnp.float32)
    out_hot = jnp.einsum("prf,fd->prd", hidden_hot, hot_down, preferred_element_type=jnp.float32)
    out_cap = out_cap.reshape(n_peer, cap_slots, count)
    outgoing = jnp.concatenate([out_cap, out_hot], axis=1).astype(jnp.bfloat16)
    returned = lax.all_to_all(outgoing, "expert", split_axis=0, concat_axis=0, tiled=True)
    back_cap = returned[:, :cap_slots].reshape(experts * CAP, width)
    back_hot = lax.dynamic_index_in_dim(returned, owner, 0, keepdims=False)[cap_slots:]
    table = jnp.concatenate([back_cap, back_hot, jnp.zeros((1, width), jnp.bfloat16)], axis=0)
    where_row = jnp.where(
        kept_cap, flat_e * CAP + rank, jnp.where(is_hot, experts * CAP + rank, experts * CAP + MOST)
    )
    picked = jnp.take(table, where_row, axis=0)
    factor = jnp.where(jnp.logical_or(kept_cap, is_hot), share, 0.0)
    summed = jnp.sum(
        (picked.astype(jnp.float32) * factor[:, None]).reshape(tok_rows, -1, width), axis=1
    )
    return summed.astype(jnp.bfloat16)


def solution(mesh):
    in_specs = (
        P(("dp", "expert"), None),
        P(("dp", "expert"), None),
        P(("dp", "expert"), None),
        P(),
        P(),
        P("expert", "dp", None),
        P("expert", "dp", None),
        P("expert", None, "dp"),
    )
    out_specs = P(("dp", "expert"), None)
    return jax.shard_map(
        per_device, mesh=mesh, in_specs=in_specs, out_specs=out_specs, check_vma=False
    )
```

profile of v0, /device:TPU:37, one launch (start us, length us, event | category | flops | bytes accessed | tf_op | source)
XLA Modules:
  0.0 495.2 jit_solution(10126614187241409905)
XLA Ops:
  12.8 2.4 convolution_convert_fusion
  15.2 3.5 reshape.158
  19.1 2.7 pad_maximum_fusion
  21.8 13.0 %all-to-all-start = ((bf16[32,32,2048]{2,1,0:T(8,128)(2,1)}), bf16[32,32,2048]{2,1,0:T(8,128)(2,1)}, u32[]{:S(2)}, u32[]{:S(2)}) async-start(bf16[32,32,2048]{2,1,0:T(8,128)(2,1)} %pad_maximum_fusion), calls=%async_computation | async-start | bytes 8388608 | tf_op jit(solution)/shard_map/all_to_all | solution.py:43
  34.9 139.3 %all-to-all-done = bf16[32,32,2048]{2,1,0:T(8,128)(2,1)} async-done(((bf16[32,32,2048]{2,1,0:T(8,128)(2,1)}), bf16[32,32,2048]{2,1,0:T(8,128)(2,1)}, u32[]{:S(2)}, u32[]{:S(2)}) %all-to-all-start) | async-done | bytes 4194336 | tf_op jit(solution)/shard_map/all_to_all | solution.py:43
  174.1 2.3 slice.31
  176.5 1.4 copy.41
  177.9 3.6 slice.32
  181.5 6.3 %fusion.4 = f32[2,32,10,768]{3,1,2,0:T(8,128)} fusion(bf16[32,2,10,2048]{3,0,2,1:T(8,128)(2,1)S(1)} %bitcast.108, bf16[2,2048,768]{2,1,0:T(8,128)(2,1)} %all-gather.4.cloned.1.call-done), kind=kOutput, calls=%fused_computation.5 | convolution fusion | flops 2013265920 | bytes 10878976 | tf_op jit(solution)/shard_map/pcrd,cdf->pcrf/dot_general | solution.py:56
  187.9 61.1 %all-gather.6.cloned.1.call-done = bf16[2,2048,768]{2,1,0:T(8,128)(2,1)} async-done(((bf16[2,256,768]{2,1,0:T(8,128)(2,1)}), bf16[2,2048,768]{2,1,0:T(8,128)(2,1)}) %all-gather.6.cloned.1.call-update) | async-done | bytes 6291472 | tf_op jit(solution)/shard_map/all_gather | solution.py:53
  248.9 75.1 %all-gather.8.cloned.1.call-done = bf16[2,768,2048]{2,1,0:T(8,128)(2,1)} async-done(((bf16[2,768,256]{2,1,0:T(8,128)(2,1)}), bf16[2,768,2048]{2,1,0:T(8,128)(2,1)}) %all-gather.8.cloned.1.call-update) | async-done | bytes 6291472 | tf_op jit(solution)/shard_map/all_gather | solution.py:65
  324.0 11.0 %fusion.6 = bf16[2,32,10,2048]{3,1,2,0:T(8,128)(2,1)} fusion(bf16[2,768,2048]{2,1,0:T(8,128)(2,1)} %all-gather.8.cloned.1.call-done, f32[2,32,10,768]{3,1,2,0:T(8,128)} %fusion.4, bf16[32,2,10,2048]{3,0,2,1:T(8,128)(2,1)S(1)} %bitcast.109, bf16[2,2048,768]{2,1,0:T(8,128)(2,1)} %all-gather.6.cloned.1.call-done), kind=kOutput, calls=%fused_computation.10 | convolution fusion | flops 4030791680 | bytes 19791872 | tf_op jit(solution)/shard_map/pcrf,cfd->pcrd/dot_general | solution.py:68
  334.9 3.3 copy.43
  338.3 5.2 %fusion.13 = f32[32,12,768]{2,0,1:T(8,128)} fusion(bf16[2,2048,768]{2,1,0:T(8,128)(2,1)} %all-gather.4.cloned.1.call-done, s32[]{:T(128)S(6)} %min.4, bf16[32,12,2048]{2,1,0:T(8,128)(2,1)S(1)} %copy-done.2), kind=kOutput, calls=%fused_computation.16 | convolution fusion | flops 1207959552 | bytes 5898244 | tf_op jit(solution)/shard_map/prd,df->prf/dot_general | solution.py:60
  343.5 8.7 %fusion.18 = bf16[32,12,2048]{2,0,1:T(8,128)(2,1)} fusion(bf16[2,768,2048]{2,1,0:T(8,128)(2,1)} %all-gather.8.cloned.1.call-done, s32[]{:T(128)S(6)} %min.4, bf16[2,2048,768]{2,1,0:T(8,128)(2,1)} %all-gather.6.cloned.1.call-done, f32[32,12,768]{2,0,1:T(8,128)} %fusion.13, bf16[32,12,2048]{2,1,0:T(8,128)(2,1)} %slice.32), kind=kOutput, calls=%fused_computation.21 | convolution fusion | flops 2418475008 | bytes 11142144 | tf_op jit(solution)/shard_map/prf,fd->prd/dot_general | solution.py:69
  352.2 2.3 copy.44
  354.5 2.6 pad_maximum_fusion.1
  357.1 9.8 %all-to-all-start.1 = ((bf16[32,32,2048]{2,1,0:T(8,128)(2,1)}), bf16[32,32,2048]{2,1,0:T(8,128)(2,1)}, u32[]{:S(2)}, u32[]{:S(2)}) async-start(bf16[32,32,2048]{2,1,0:T(8,128)(2,1)} %pad_maximum_fusion.1), calls=%async_computation.1 | async-start | bytes 8388608 | tf_op jit(solution)/shard_map/all_to_all | solution.py:72
  367.6 105.7 %all-to-all-done.1 = bf16[32,32,2048]{2,1,0:T(8,128)(2,1)} async-done(((bf16[32,32,2048]{2,1,0:T(8,128)(2,1)}), bf16[32,32,2048]{2,1,0:T(8,128)(2,1)}, u32[]{:S(2)}, u32[]{:S(2)}) %all-to-all-start.1) | async-done | bytes 4194336 | tf_op jit(solution)/shard_map/all_to_all | solution.py:72
  473.3 2.1 slice.33
  475.4 2.2 reshape.161
  478.5 2.2 maximum_maximum_fusion
  480.8 3.3 gather_fusion
  484.1 4.5 multiply_reduce_fusion
  (45 shorter events, 7.3 us)
Async XLA Ops:
  6.5 6.3 %copy-start = (bf16[64,2048]{1,0:T(8,128)(2,1)S(1)}, bf16[64,2048]{1,0:T(8,128)(2,1)}, u32[]{:S(2)}) copy-start(bf16[64,2048]{1,0:T(8,128)(2,1)} %param.8) | copy-start | bytes 786436
  6.5 5.3 %copy-start.4 = (s32[64]{0:T(128)S(1)}, s32[64]{0:T(128)}, u32[]{:S(2)}) copy-start(s32[64]{0:T(128)} %param.11) | copy-start | bytes 772
  6.5 175.0 %all-gather.4.cloned.1.call-start = ((), (), s32[]{:S(2)}) async-start(), calls=%async_computation.2 | async-start | bytes 7077888 | tf_op jit(solution)/shard_map/all_gather | solution.py:52
  7.3 241.6 %all-gather.6.cloned.1.call-start = ((), (), s32[]{:S(2)}) async-start(), calls=%async_computation.3 | async-start | bytes 7077888 | tf_op jit(solution)/shard_map/all_gather | solution.py:53
  8.0 315.9 %all-gather.8.cloned.1.call-start = ((), (), s32[]{:S(2)}) async-start(), calls=%async_computation.4 | async-start | bytes 7077888 | tf_op jit(solution)/shard_map/all_gather | solution.py:65
  21.8 152.3 %all-to-all-start = ((bf16[32,32,2048]{2,1,0:T(8,128)(2,1)}), bf16[32,32,2048]{2,1,0:T(8,128)(2,1)}, u32[]{:S(2)}, u32[]{:S(2)}) async-start(bf16[32,32,2048]{2,1,0:T(8,128)(2,1)} %pad_maximum_fusion), calls=%async_computation | async-start | bytes 8388608 | tf_op jit(solution)/shard_map/all_to_all | solution.py:43
  334.9 3.4 copy-start.2
  357.1 10.0 %copy-start.3 = (s32[64,8]{0,1:T(8,128)S(1)}, s32[64,8]{0,1:T(8,128)}, u32[]{:S(2)}) copy-start(s32[64,8]{0,1:T(8,128)} %param.10) | copy-start | bytes 6148
  357.1 116.2 %all-to-all-start.1 = ((bf16[32,32,2048]{2,1,0:T(8,128)(2,1)}), bf16[32,32,2048]{2,1,0:T(8,128)(2,1)}, u32[]{:S(2)}, u32[]{:S(2)}) async-start(bf16[32,32,2048]{2,1,0:T(8,128)(2,1)} %pad_maximum_fusion.1), calls=%async_computation.1 | async-start | bytes 8388608 | tf_op jit(solution)/shard_map/all_to_all | solution.py:72
  480.8 7.9 %copy-start.1 = (bf16[64,2048]{1,0:T(8,128)(2,1)S(1)}, bf16[64,2048]{1,0:T(8,128)(2,1)}, u32[]{:S(2)}) copy-start(bf16[64,2048]{1,0:T(8,128)(2,1)} %param.8) | copy-start | bytes 786436
Sparse Core Ops, SparseCore 0:
  9.1 164.8 all-gather.3
  175.8 73.0 all-gather.5
  250.6 73.2 all-gather.7
where the time goes:
time: 496 us; the launch traced here: 495 us
  waiting for transfers between devices  383 us (77%)
  matrix products  33.7 us (7%)
  local copies, waits for them, and re-layouts  26.9 us (5%)
  starting transfers between devices  23 us (5%)
  other arithmetic  14.4 us (3%)
  between operations  14 us (3%)
    all_to_all x1, waiting for transfers between devices, per_device(): lax.all_to_all(jnp.concatenate([send_cap, send_hot], axis=1), 'expert', s...  139 us
    all_to_all x1, waiting for transfers between devices, per_device(): lax.all_to_all(outgoing, 'expert', split_axis=0, concat_axis=0, tiled=True)  106 us
    all_gather x1, waiting for transfers between devices, per_device(): piece = lax.all_gather(w_down, 'dp', axis=2, tiled=True)  75.1 us
    all_gather x1, waiting for transfers between devices, per_device(): piece_up = lax.all_gather(w_up, 'dp', axis=1, tiled=True)  61.1 us
    all_to_all x1, starting transfers between devices, per_device(): lax.all_to_all(jnp.concatenate([send_cap, send_hot], axis=1), 'expert', s...  13 us
    dot_general x1, matrix products, per_device(): jnp.einsum('pcrf,cfd->pcrd', hidden_cap, piece, preferred_element_type=jn...  11 us
  transfers between devices with their start and end apart: 5, of which 4 were waited for; matrix products, arithmetic and copies ran while one was open for 5% of the time, Pallas kernels for 0%

commit v1 on v0

--- a/solution.py
+++ b/solution.py
@@ -50,7 +50,8 @@
     recv_cap = received[:, :cap_slots].reshape(n_peer, exp_dev, CAP, width)
     recv_hot = received[:, cap_slots:]
     piece_gate = lax.all_gather(w_gate, "dp", axis=1, tiled=True)
-    piece_up = lax.all_gather(w_up, "dp", axis=1, tiled=True)
+    sent = jnp.stack([w_up] * lax.axis_size("dp"))
+    piece_up = jnp.concatenate(lax.all_to_all(sent, "dp", 0, 0), axis=1)
     hot_gate = lax.dynamic_index_in_dim(piece_gate, hot_local, 0, keepdims=False)
     hot_up = lax.dynamic_index_in_dim(piece_up, hot_local, 0, keepdims=False)
     gate_cap = jnp.einsum(

time: 496 us -> 556 us (1.12)
  the two profiles are of different devices: /device:TPU:37 before, /device:TPU:64 now
where the time goes in v1:
time: 556 us; the launch traced here: 555 us
  waiting for transfers between devices  291 us (52%)
  blocking collectives  157 us (28%)
  local copies, waits for them, and re-layouts  34.2 us (6%)
  matrix products  34 us (6%)
  between operations  14.3 us (3%)
  other arithmetic  14 us (3%)
  starting transfers between devices  10.3 us (2%)
    all_to_all x1, waiting for transfers between devices, per_device(): piece_up = jnp.concatenate(lax.all_to_all(sent, 'dp', 0, 0), axis=1)  188 us
    all_to_all x1, blocking collectives, per_device(): lax.all_to_all(jnp.concatenate([send_cap, send_hot], axis=1), 'expert', s...  157 us
    all_to_all x1, waiting for transfers between devices, per_device(): lax.all_to_all(outgoing, 'expert', split_axis=0, concat_axis=0, tiled=True)  101 us
    dot_general x1, matrix products, per_device(): jnp.einsum('pcrf,cfd->pcrd', hidden_cap, piece, preferred_element_type=jn...  12 us
  transfers between devices with their start and end apart: 4, of which 2 were waited for; matrix products, arithmetic and copies ran while one was open for 5% of the time, Pallas kernels for 0%

profile of v1, /device:TPU:64, one launch (start us, length us, event | category | flops | bytes accessed | tf_op | source)
XLA Modules:
  0.0 554.9 jit_solution(11819927315363037683)
XLA Ops:
  12.0 2.4 convolution_convert_fusion
  14.4 3.5 reshape.166
  18.4 1.5 pad_maximum_fusion
  19.9 157.2 %all_to_all.15 = bf16[32,32,2048]{2,1,0:T(8,128)(2,1)} all-to-all(bf16[32,32,2048]{2,1,0:T(8,128)(2,1)S(1)} %pad_maximum_fusion), channel_id=1, replica_groups=mesh['dp'=8,'expert'=32] {'expert'}, dimensions={0} | all-to-all | bytes 8388608 | tf_op jit(solution)/shard_map/all_to_all | solution.py:43
  177.0 3.2 stack.2
  180.3 5.3 all-to-all-start.1
  186.3 1.9 slice-done
  188.2 2.9 copy.42
  191.8 188.4 %all-to-all-done.1 = bf16[8,2,256,768]{3,2,1,0:T(8,128)(2,1)} async-done(((bf16[8,2,256,768]{3,2,1,0:T(8,128)(2,1)}), bf16[8,2,256,768]{3,2,1,0:T(8,128)(2,1)}, u32[]{:S(2)}, u32[]{:S(2)}) %all-to-all-start.1) | async-done | bytes 6291488 | tf_op jit(solution)/shard_map/all_to_all | solution.py:54
  380.2 6.0 %copy.43 = bf16[8,2,256,768]{3,2,0,1:T(8,128)(2,1)} copy(bf16[8,2,256,768]{3,2,1,0:T(8,128)(2,1)} %all-to-all-done.1) | data formatting | bytes 12582912 | tf_op jit(solution)/shard_map/all_to_all | solution.py:54
  386.1 5.2 fusion.11
  391.3 7.9 %fusion.16 = bf16[32,12,2048]{2,0,1:T(8,128)(2,1)} fusion(bf16[2,768,2048]{2,1,0:T(8,128)(2,1)} %all-gather.5.cloned.1.call-done, s32[]{:T(128)S(6)} %min.4, bf16[2,2048,768]{2,1,0:T(8,128)(2,1)} %bitcast.107, f32[32,12,768]{2,0,1:T(8,128)} %fusion.11, bf16[32,12,2048]{2,1,0:T(8,128)(2,1)S(1)} %slice.32), kind=kOutput, calls=%fused_computation.19 | convolution fusion | flops 2418475008 | bytes 10617856 | tf_op jit(solution)/shard_map/prf,fd->prd/dot_general | solution.py:70
  399.2 2.4 copy.46
  401.7 6.3 %fusion.2 = f32[2,32,10,768]{3,1,2,0:T(8,128)} fusion(bf16[32,2,10,2048]{3,0,2,1:T(8,128)(2,1)S(1)} %bitcast.110, bf16[2,2048,768]{2,1,0:T(8,128)(2,1)} %all-gather.3.cloned.1.call-done), kind=kOutput, calls=%fused_computation.3 | convolution fusion | flops 2013265920 | bytes 10878976 | tf_op jit(solution)/shard_map/pcrd,cdf->pcrf/dot_general | solution.py:57
  408.0 12.0 %fusion.4 = bf16[2,32,10,2048]{3,1,2,0:T(8,128)(2,1)} fusion(bf16[2,768,2048]{2,1,0:T(8,128)(2,1)} %all-gather.5.cloned.1.call-done, f32[2,32,10,768]{3,1,2,0:T(8,128)} %fusion.2, bf16[32,2,10,2048]{3,0,2,1:T(8,128)(2,1)} %bitcast.109, bf16[2,2048,768,1]{2,1,3,0:T(8,128)(2,1)} %bitcast.108), kind=kOutput, calls=%fused_computation.8 | convolution fusion | flops 4030791680 | bytes 19791872 | tf_op jit(solution)/shard_map/pcrf,cfd->pcrd/dot_general | solution.py:69
  420.0 3.2 copy.45
  423.2 2.7 pad_maximum_fusion.1
  425.9 5.0 all-to-all-start.2
  431.5 101.2 %all-to-all-done.2 = bf16[32,32,2048]{2,1,0:T(8,128)(2,1)} async-done(((bf16[32,32,2048]{2,1,0:T(8,128)(2,1)}), bf16[32,32,2048]{2,1,0:T(8,128)(2,1)}, u32[]{:S(2)}, u32[]{:S(2)}) %all-to-all-start.2) | async-done | bytes 4194336 | tf_op jit(solution)/shard_map/all_to_all | solution.py:73
  532.7 2.1 slice.33
  534.8 2.2 reshape.171
  537.9 2.2 maximum_maximum_fusion
  540.2 3.3 gather_fusion
  543.5 4.5 multiply_reduce_fusion
  (48 shorter events, 7.9 us)
Async XLA Ops:
  6.5 5.4 copy-start
  6.5 379.6 %all-gather.3.cloned.1.call-start = ((), (), s32[]{:S(2)}) async-start(), calls=%async_computation.3 | async-start | bytes 7077888 | tf_op jit(solution)/shard_map/all_gather | solution.py:52
  19.8 157.2 %copy-start.4 = (bf16[2,256,768]{2,1,0:T(8,128)(2,1)S(1)}, bf16[2,256,768]{2,1,0:T(8,128)(2,1)}, u32[]{:S(2)}) copy-start(bf16[2,256,768]{2,1,0:T(8,128)(2,1)} %param.14) | copy-start | bytes 2359300
  180.3 199.9 %all-to-all-start.1 = ((bf16[8,2,256,768]{3,2,1,0:T(8,128)(2,1)}), bf16[8,2,256,768]{3,2,1,0:T(8,128)(2,1)}, u32[]{:S(2)}, u32[]{:S(2)}) async-start(bf16[8,2,256,768]{3,2,1,0:T(8,128)(2,1)} %stack.2), calls=%async_computation.1 | async-start | bytes 12582912 | tf_op jit(solution)/shard_map/all_to_all | solution.py:54
  185.5 205.8 %all-gather.5.cloned.1.call-start = ((), (), s32[]{:S(2)}) async-start(), calls=%async_computation.4 | async-start | bytes 7077888 | tf_op jit(solution)/shard_map/all_gather | solution.py:66
  186.3 1.9 slice-start
  188.2 2.9 copy-start.2
  399.2 2.5 copy-start.3
  425.9 5.1 copy-start.5
  425.9 106.8 %all-to-all-start.2 = ((bf16[32,32,2048]{2,1,0:T(8,128)(2,1)}), bf16[32,32,2048]{2,1,0:T(8,128)(2,1)}, u32[]{:S(2)}, u32[]{:S(2)}) async-start(bf16[32,32,2048]{2,1,0:T(8,128)(2,1)} %pad_maximum_fusion.1), calls=%async_computation.2 | async-start | bytes 8388608 | tf_op jit(solution)/shard_map/all_to_all | solution.py:73
  540.2 7.9 %copy-start.1 = (bf16[64,2048]{1,0:T(8,128)(2,1)S(1)}, bf16[64,2048]{1,0:T(8,128)(2,1)}, u32[]{:S(2)}) copy-start(bf16[64,2048]{1,0:T(8,128)(2,1)} %param.8) | copy-start | bytes 786436
Sparse Core Ops, SparseCore 0:
  9.1 162.8 all-gather.2
  188.1 191.8 all-gather.4
